TPU v7x, 32 devices: a whole 2x2x4 slice. The times are simulated.
32 devices in a mesh: parts: 2 (over y), row: 4 (over z), col: 4 (over x, core).
Axes of the slice: x: 2, y: 2, z: 4, core: 2. Of those that a mesh axis runs over, the one named last changes fastest.
Arguments:
- sigma_anc: float32 [24576, 12288], P(('parts', 'row'), 'col'), parts along dimension 0
- normal_factor: float32 [4, 12288, 512], P('parts', ('col', 'row')), parts along dimension 0, may hold values from -0.078125 to 0.078125
- jj_inverse: float32 [4, 512, 512], P('parts', None, 'col'), parts along dimension 0, may hold values from -6 to 6
- blocks: int32 [4, 128], P('parts'), parts along dimension 0, may hold values from 0 to 255, as said below
Outputs:
- sigma_rj: float32 [4, 12288, 512], P('parts', 'row', 'col'), parts along dimension 0
- sigma_jj: float32 [4, 512, 512], P('parts', None, 'col'), parts along dimension 0
There are 2 independent parts, one for each index of `parts`. A program takes and returns all parts, laid end to end along the dimension named above; each array names one. Nothing has to cross between parts.
Inputs may be any that keep to these rules, and one draw needn't show every extreme that they name: Each list names 128 different blocks and always holds block 0 and block 255.
All inputs are finite; a program needn't handle non-finite values.
Results may differ from a plain program's by a relative error of at most 0.0001.
Values sent between devices are 32-bit elements; how exact they have to be, the bound alone decides.
A program may use at most 192 MiB of HBM per device.

v0:
```python
import jax
import jax.numpy as jnp
from jax import lax
from jax.sharding import PartitionSpec as P

BLK = 48


def listed_mask(blocks, first_block, count, rows):
    block_ids = first_block + jnp.arange(count, dtype=jnp.int32)
    listed = jnp.any(blocks[:, :, None] == block_ids[None, None, :], axis=1).astype(jnp.float32)
    return jnp.repeat(listed, BLK, axis=1, total_repeat_length=rows)[:, :, None]


def shards(sigma_anc, normal_factor, jj_inverse, blocks):
    tile_rows, tile_cols = sigma_anc.shape
    row_count = lax.axis_size("row")
    row_index = lax.axis_index("row")
    col_index = lax.axis_index("col")
    local_rows = normal_factor.shape[1]
    local_blocks = local_rows // BLK
    first_local = (col_index * row_count + row_index) * local_blocks
    masked = normal_factor * listed_mask(blocks, first_local, local_blocks, local_rows)
    row_blocks = tile_rows // BLK
    row_mask = listed_mask(blocks, row_index * row_blocks, row_blocks, tile_rows)
    start_row = row_index * tile_rows
    root_col = start_row // tile_cols
    offset = jnp.clip(start_row - col_index * tile_cols, 0, tile_cols - tile_rows)
    is_root = (col_index == root_col).astype(jnp.float32)
    rj_list = []
    update_list = []
    for supernode in range(2):
        gathered = lax.all_gather(masked[supernode], "row", axis=0, tiled=True)
        partial = jnp.dot(
            sigma_anc, gathered, precision=lax.Precision.HIGH, preferred_element_type=jnp.float32
        )
        own_rj = -lax.psum_scatter(
            partial * row_mask[supernode], "col", scatter_dimension=1, tiled=True
        )
        rj_list.append(own_rj)
        wide_rj = lax.all_gather(own_rj, "col", axis=1, tiled=True)
        slab = lax.dynamic_slice_in_dim(gathered, offset, tile_rows, 0) * is_root
        update = lax.dot_general(
            slab,
            wide_rj,
            (((0,), (0,)), ((), ())),
            precision=lax.Precision.HIGH,
            preferred_element_type=jnp.float32,
        )
        update_list.append(
            lax.psum(lax.psum_scatter(update, "col", scatter_dimension=1, tiled=True), "row")
        )
    return (jnp.stack(rj_list), jj_inverse - jnp.stack(update_list))


def solution(mesh):
    placed = (
        P(("parts", "row"), "col"),
        P("parts", ("col", "row"), None),
        P("parts", None, "col"),
        P("parts", None),
    )
    return jax.shard_map(
        shards,
        mesh=mesh,
        in_specs=placed,
        out_specs=(P("parts", "row", "col"), P("parts", None, "col")),
        check_vma=False,
    )
```

profile of v0, /device:TPU:0, one launch (start us, length us, event | category | flops | bytes accessed | tf_op | source)
XLA Modules:
  0.0 573.0 jit_solution(10979280178893593499)
XLA Ops:
  7.2 0.0 all-gather.11.cloned.1.call-start
  7.2 0.9 compare_reduce_fusion.1
  8.1 0.1 copy.10
  8.2 0.7 pad_clamp_fusion
  8.9 1.6 gather_fusion
  10.5 0.1 copy.11
  10.6 2.2 broadcast_multiply_fusion
  12.8 0.0 copy-start
  12.8 2.0 fusion.12
  14.8 0.0 all-gather.11.cloned.1.call-update
  14.8 0.0 all-gather.13.cloned.1.call-start
  14.9 0.7 all-gather.13.cloned.1.call-update
  15.6 0.0 reduce-scatter.5.cloned.1.call-start
  15.6 0.2 compare_reduce_fusion
  15.8 0.1 copy.12
  15.9 8.1 %gather_fusion.1 = f32[3072,2]{1,0:T(8,128)S(1)} fusion(f32[2,64]{0,1:T(8,128)S(1)} %copy.12, s32[3072]{0:T(1024)S(1)} %broadcast_clamp_fusion), kind=kCustom, calls=%fused_computation.1 | custom fusion | bytes 61440 | tf_op jit(solution)/shard_map/jit(_take)/gather | solution.py:12
  24.1 1.3 slice_reduce_fusion.1
  25.4 107.6 %all-gather.11.cloned.1.call-done = f32[1,3072,512]{2,1,0:T(8,128)} async-done(((f32[1,768,512]{2,1,0:T(8,128)}), f32[1,3072,512]{2,1,0:T(8,128)}) %all-gather.11.cloned.1.call-update) | async-done | bytes 6291472 | tf_op jit(solution)/shard_map/all_gather | solution.py:33
  133.0 66.4 %multiply_bitcast_fusion.1 = f32[3072,512]{0,1:T(8,128)} fusion(f32[3072,3072]{1,0:T(8,128)} %param.8, f32[1,3072,512]{2,1,0:T(8,128)} %all-gather.11.cloned.1.call-done, f32[3072]{0:T(1024)S(1)} %get-tuple-element.32), kind=kOutput, calls=%fused_computation.11 | convolution fusion | flops 28992602112 | bytes 50343936 | tf_op jit(solution)/shard_map/dot_general | solution.py:34
  199.4 0.0 reduce-scatter.5.cloned.1.call-update
  199.5 0.0 reduce-scatter.7.cloned.1.call-start
  199.5 48.7 %all-gather.13.cloned.1.call-done = f32[1,3072,512]{2,1,0:T(8,128)} async-done(((f32[1,768,512]{2,1,0:T(8,128)}), f32[1,3072,512]{2,1,0:T(8,128)}) %all-gather.13.cloned.1.call-update) | async-done | bytes 6291472 | tf_op jit(solution)/shard_map/all_gather | solution.py:33
  248.2 66.4 %multiply_bitcast_fusion = f32[3072,512]{0,1:T(8,128)} fusion(f32[3072,3072]{1,0:T(8,128)} %param.8, f32[1,3072,512]{2,1,0:T(8,128)} %all-gather.13.cloned.1.call-done, f32[3072]{0:T(1024)S(1)} %get-tuple-element.33), kind=kOutput, calls=%fused_computation.10 | convolution fusion | flops 28992602112 | bytes 50343936 | tf_op jit(solution)/shard_map/dot_general | solution.py:34
  314.6 0.0 reduce-scatter.7.cloned.1.call-update
  314.6 0.0 all-gather.7.cloned.1.call-start
  314.7 0.0 reduce-scatter.5.cloned.1.call-done
  314.7 3.5 fusion.13
  318.2 0.0 all-gather.7.cloned.1.call-update
  318.2 0.0 all-gather.9.cloned.1.call-start
  318.3 53.1 %reduce-scatter.7.cloned.1.call-done = f32[3072,128]{0,1:T(8,128)} async-done(((f32[3072,512]{0,1:T(8,128)}), f32[3072,128]{0,1:T(8,128)}) %reduce-scatter.7.cloned.1.call-update) | async-done | bytes 1572880 | tf_op jit(solution)/shard_map/reduce_scatter | solution.py:37
  371.4 3.4 fusion.14
  374.8 0.0 all-gather.9.cloned.1.call-update
  374.8 0.0 reduce-scatter.9.cloned.1.call-start
  374.9 44.3 %all-gather.7.cloned.1.call-done = f32[3072,512]{0,1:T(8,128)} async-done(((f32[3072,128]{0,1:T(8,128)}), f32[3072,512]{0,1:T(8,128)}) %all-gather.7.cloned.1.call-update) | async-done | bytes 6291472 | tf_op jit(solution)/shard_map/all_gather | solution.py:41
  419.2 14.7 %fusion.5 = f32[512,512]{1,0:T(8,128)} fusion(f32[3072,512]{0,1:T(8,128)} %all-gather.7.cloned.1.call-done, f32[1,3072,512]{2,1,0:T(8,128)} %all-gather.11.cloned.1.call-done, f32[]{:T(128)S(6)} %convert_element_type.11), kind=kOutput, calls=%fused_computation.9 | convolution fusion | flops 4833411072 | bytes 13631492 | tf_op jit(solution)/shard_map/dot_general | solution.py:43
  433.9 0.0 reduce-scatter.9.cloned.1.call-update
  433.9 0.0 reduce-scatter.11.cloned.1.call-start
  434.0 33.7 %all-gather.9.cloned.1.call-done = f32[3072,512]{0,1:T(8,128)} async-done(((f32[3072,128]{0,1:T(8,128)}), f32[3072,512]{0,1:T(8,128)}) %all-gather.9.cloned.1.call-update) | async-done | bytes 6291472 | tf_op jit(solution)/shard_map/all_gather | solution.py:41
  467.6 14.6 %fusion.2 = f32[512,512]{1,0:T(8,128)} fusion(f32[3072,512]{0,1:T(8,128)} %all-gather.9.cloned.1.call-done, f32[1,3072,512]{2,1,0:T(8,128)} %all-gather.13.cloned.1.call-done, f32[]{:T(128)S(6)} %convert_element_type.11), kind=kOutput, calls=%fused_computation.5 | convolution fusion | flops 4833411072 | bytes 13631492 | tf_op jit(solution)/shard_map/dot_general | solution.py:43
  482.3 0.0 reduce-scatter.11.cloned.1.call-update
  482.3 0.0 all-reduce.3.cloned.1.call-start
  482.3 12.8 %reduce-scatter.9.cloned.1.call-done = f32[512,128]{1,0:T(8,128)} async-done(((f32[512,512]{1,0:T(8,128)}), f32[512,128]{1,0:T(8,128)}) %reduce-scatter.9.cloned.1.call-update) | async-done | bytes 262160 | tf_op jit(solution)/shard_map/reduce_scatter | solution.py:51
  495.1 28.2 %reduce-scatter.11.cloned.1.call-done = f32[512,128]{1,0:T(8,128)} async-done(((f32[512,512]{1,0:T(8,128)}), f32[512,128]{1,0:T(8,128)}) %reduce-scatter.11.cloned.1.call-update) | async-done | bytes 262160 | tf_op jit(solution)/shard_map/reduce_scatter | solution.py:51
  523.3 0.0 all-reduce.3.cloned.1.call-update
  523.3 2.1 pad_maximum_fusion
  525.4 2.4 copy.13
  527.8 36.4 %all-reduce.3.cloned.1.call-done = (f32[1,512,128]{2,1,0:T(8,128)}, f32[1,512,128]{2,1,0:T(8,128)}) async-done(((f32[1,512,128]{2,1,0:T(8,128)}, f32[1,512,128]{2,1,0:T(8,128)}), (f32[1,512,128]{2,1,0:T(8,128)}, f32[1,512,128]{2,1,0:T(8,128)})) %all-reduce.3.cloned.1.call-update) | async-done | bytes 524304 | tf_op jit(solution)/shard_map/psum | solution.py:51
  564.2 2.0 maximum_subtract_fusion
  (8 shorter events, 0.0 us)
Async XLA Ops:
  7.2 125.8 %all-gather.11.cloned.1.call-start = ((), (), s32[]{:S(2)}) async-start(), calls=%async_computation.10 | async-start | bytes 7864320 | tf_op jit(solution)/shard_map/all_gather | solution.py:33
  12.8 2.8 copy-start.1
  12.8 3.1 copy-start
  14.8 233.4 %all-gather.13.cloned.1.call-start = ((), (), s32[]{:S(2)}) async-start(), calls=%async_computation.11 | async-start | bytes 7864320 | tf_op jit(solution)/shard_map/all_gather | solution.py:33
  15.6 299.2 %reduce-scatter.5.cloned.1.call-start = ((), (), s32[]{:S(2)}) async-start(), calls=%async_computation.4 | async-start | bytes 7864320 | tf_op jit(solution)/shard_map/reduce_scatter | solution.py:37
  199.5 171.9 %reduce-scatter.7.cloned.1.call-start = ((), (), s32[]{:S(2)}) async-start(), calls=%async_computation.5 | async-start | bytes 7864320 | tf_op jit(solution)/shard_map/reduce_scatter | solution.py:37
  314.6 104.6 %all-gather.7.cloned.1.call-start = ((), (), s32[]{:S(2)}) async-start(), calls=%async_computation.6 | async-start | bytes 7864320 | tf_op jit(solution)/shard_map/all_gather | solution.py:41
  318.2 149.4 %all-gather.9.cloned.1.call-start = ((), (), s32[]{:S(2)}) async-start(), calls=%async_computation.8 | async-start | bytes 7864320 | tf_op jit(solution)/shard_map/all_gather | solution.py:41
  374.8 120.3 %reduce-scatter.9.cloned.1.call-start = ((), (), s32[]{:S(2)}) async-start(), calls=%async_computation.7 | async-start | bytes 1310720 | tf_op jit(solution)/shard_map/reduce_scatter | solution.py:51
  433.9 89.4 %reduce-scatter.11.cloned.1.call-start = ((), (), s32[]{:S(2)}) async-start(), calls=%async_computation.9 | async-start | bytes 1310720 | tf_op jit(solution)/shard_map/reduce_scatter | solution.py:51
  482.3 81.9 %all-reduce.3.cloned.1.call-start = ((), (), s32[]{:S(2)}) async-start(), calls=%async_computation.12 | async-start | bytes 1048576 | tf_op jit(solution)/shard_map/psum | solution.py:51
Sparse Core Ops, SparseCore 0:
  14.9 118.0 all-gather.10
  134.6 113.5 all-gather.12
  250.7 56.5 reduce-scatter.4
  314.8 56.5 reduce-scatter.6
  372.8 46.3 all-gather.6
  421.2 46.3 all-gather.8
  470.1 24.9 reduce-scatter.8
  498.4 24.8 reduce-scatter.10
  525.7 38.4 all-reduce.2
where the time goes:
time: 576 us; the launch traced here: 573 us
  waiting for transfers between devices  366 us (64%)
  matrix products  162 us (28%)
  local copies, waits for them, and re-layouts  15.7 us (3%)
  other arithmetic  15 us (3%)
  between operations  14.2 us (2%)
    all_gather x2, waiting for transfers between devices, shards(): gathered = lax.all_gather(masked[supernode], 'row', axis=0, tiled=True)  156 us
    dot_general x2, matrix products, shards(): jnp.dot(sigma_anc, gathered, precision=lax.Precision.HIGH, preferred_elem...  133 us
    all_gather x2, waiting for transfers between devices, shards(): wide_rj = lax.all_gather(own_rj, 'col', axis=1, tiled=True)  78 us
    reduce_scatter x2, waiting for transfers between devices, shards(): lax.psum_scatter(partial * row_mask[supernode], 'col', scatter_dimension=...  53.1 us
    reduce_scatter x2, waiting for transfers between devices, shards(): lax.psum_scatter(update, 'col', scatter_dimension=1, tiled=True)  41 us
    psum x1, waiting for transfers between devices, shards(): lax.psum(lax.psum_scatter(update, 'col', scatter_dimension=1, tiled=True)...  36.4 us
    dot_general x2, matrix products, shards(): lax.dot_general(slab, wide_rj, (((0,), (0,)), ((), ())), precision=lax.Pr...  29.3 us
  transfers between devices with their start and end apart: 9, of which 8 were waited for; matrix products, arithmetic and copies ran while one was open for 32% of the time, Pallas kernels for 0%

commit v1 on v0

--- a/solution.py
+++ b/solution.py
@@ -30,7 +30,14 @@
     rj_list = []
     update_list = []
     for supernode in range(2):
-        gathered = lax.all_gather(masked[supernode], "row", axis=0, tiled=True)
+        ring = [masked[supernode]]
+        for hop in range(3):
+            ring.append(lax.ppermute(ring[-1], "row", [(dev, (dev + 1) % 4) for dev in range(4)]))
+        gathered = jnp.roll(
+            jnp.concatenate(ring[::-1], axis=0),
+            (lax.axis_index("row") + 1) * ring[0].shape[0],
+            axis=0,
+        )
         partial = jnp.dot(
             sigma_anc, gathered, precision=lax.Precision.HIGH, preferred_element_type=jnp.float32
         )

time: 576 us -> 671 us (1.16)
  waiting for transfers between devices: 366 us -> 411 us
  other arithmetic: 15 us -> 37.9 us
  matrix products: 162 us -> 176 us
  local copies, waits for them, and re-layouts: 15.7 us -> 22.7 us
    ppermute x0 -> x6, waiting for transfers between devices: none -> 204 us  [shards(): lax.ppermute(ring[-1], 'row', [(dev, (dev + 1) % 4) for dev in range(4)])]
    all_gather x2 -> x0, waiting for transfers between devices: 156 us -> none  [shards(): gathered = lax.all_gather(masked[supernode], 'row', axis=0, tiled=True)]
    concatenate x0 -> x2, other arithmetic: none -> 22.6 us  [shards(): jnp.roll(jnp.concatenate(ring[::-1], axis=0), (lax.axis_index('row') + 1)...]
    dot_general x2, matrix products: 133 us -> 146 us  [shards(): jnp.dot(sigma_anc, gathered, precision=lax.Precision.HIGH, preferred_elem...]
    unnamed x5 -> x15, local copies, waits for them, and re-layouts: 2.37 us -> 11.1 us
  transfers between devices with their start and end apart: 9 -> 13, of which waited for: 8 -> 12; matrix products, arithmetic and copies ran while one was open for 32% -> 19% of each run, Pallas kernels for 0% -> 0%
where the time goes in v1:
time: 671 us; the launch traced here: 665 us
  waiting for transfers between devices  411 us (61%)
  matrix products  176 us (26%)
  other arithmetic  37.9 us (6%)
  local copies, waits for them, and re-layouts  22.7 us (3%)
  between operations  14.7 us (2%)
    ppermute x6, waiting for transfers between devices, shards(): lax.ppermute(ring[-1], 'row', [(dev, (dev + 1) % 4) for dev in range(4)])  204 us
    dot_general x2, matrix products, shards(): jnp.dot(sigma_anc, gathered, precision=lax.Precision.HIGH, preferred_elem...  146 us
    all_gather x2, waiting for transfers between devices, shards(): wide_rj = lax.all_gather(own_rj, 'col', axis=1, tiled=True)  78.1 us
    reduce_scatter x2, waiting for transfers between devices, shards(): lax.psum_scatter(partial * row_mask[supernode], 'col', scatter_dimension=...  51.8 us
    reduce_scatter x2, waiting for transfers between devices, shards(): lax.psum_scatter(update, 'col', scatter_dimension=1, tiled=True)  40.7 us
    psum x1, waiting for transfers between devices, shards(): lax.psum(lax.psum_scatter(update, 'col', scatter_dimension=1, tiled=True)...  36.4 us
    dot_general x2, matrix products, shards(): lax.dot_general(slab, wide_rj, (((0,), (0,)), ((), ())), precision=lax.Pr...  29.3 us
    concatenate x2, other arithmetic, shards(): jnp.roll(jnp.concatenate(ring[::-1], axis=0), (lax.axis_index('row') + 1)...  22.6 us
  transfers between devices with their start and end apart: 13, of which 12 were waited for; matrix products, arithmetic and copies ran while one was open for 19% of the time, Pallas kernels for 0%

profile of v1, /device:TPU:0, one launch (start us, length us, event | category | flops | bytes accessed | tf_op | source)
XLA Modules:
  0.0 665.3 jit_solution(18407191615659276135)
XLA Ops:
  7.2 0.0 reduce-scatter.5.cloned.1.call-start
  7.2 0.9 compare_reduce_fusion.1
  8.1 0.1 copy.10
  8.2 0.7 pad_clamp_fusion
  8.9 1.6 gather_fusion
  10.5 0.1 copy.11
  10.6 2.2 broadcast_multiply_fusion
  12.8 0.3 slice_bitcast_fusion.1
  13.1 1.2 copy-done.2
  14.3 3.0 collective-permute-start
  17.3 36.4 %collective-permute-done = f32[768,512]{1,0:T(8,128)S(1)} collective-permute-done((f32[768,512]{1,0:T(8,128)S(1)}, f32[768,512]{1,0:T(8,128)S(1)}, u32[]{:S(2)}, u32[]{:S(2)}) %collective-permute-start) | collective-permute-done | bytes 1572896 | tf_op jit(solution)/shard_map/ppermute | solution.py:35
  53.7 1.1 copy-done.3
  54.9 37.5 %collective-permute-done.1 = f32[768,512]{1,0:T(8,128)} collective-permute-done((f32[768,512]{1,0:T(8,128)S(1)}, f32[768,512]{1,0:T(8,128)}, u32[]{:S(2)}, u32[]{:S(2)}) %collective-permute-start.1) | collective-permute-done | bytes 1572896 | tf_op jit(solution)/shard_map/ppermute | solution.py:35
  92.4 0.2 compare_reduce_fusion
  92.5 0.1 copy.12
  92.7 8.1 %gather_fusion.1 = f32[3072,2]{1,0:T(8,128)S(1)} fusion(f32[2,64]{0,1:T(8,128)S(1)} %copy.12, s32[3072]{0:T(1024)S(1)} %broadcast_clamp_fusion), kind=kCustom, calls=%fused_computation.1 | custom fusion | bytes 61440 | tf_op jit(solution)/shard_map/jit(_take)/gather | solution.py:12
  100.8 1.3 slice_reduce_fusion.1
  102.1 27.0 %collective-permute-done.2 = f32[768,512]{1,0:T(8,128)} collective-permute-done((f32[768,512]{1,0:T(8,128)}, f32[768,512]{1,0:T(8,128)}, u32[]{:S(2)}, u32[]{:S(2)}) %collective-permute-start.2) | collective-permute-done | bytes 1572896 | tf_op jit(solution)/shard_map/ppermute | solution.py:35
  129.1 10.5 %fusion.10 = f32[3072,512]{1,0:T(8,128)S(1)} fusion(s32[]{:T(128)S(6)} %select_n.56, f32[768,512]{1,0:T(8,128)} %collective-permute-done.2, f32[768,512]{1,0:T(8,128)} %collective-permute-done.1, f32[768,512]{1,0:T(8,128)} %copy-done.3, f32[768,512]{1,0:T(8,128)} %copy-done.2), kind=kLoop, calls=%fused_computation.28 | loop fusion | flops 11010048 | bytes 12582916 | tf_op jit(solution)/shard_map/jit(_roll_dynamic)/concatenate | solution.py:36
  139.6 2.6 copy-done
  142.3 80.1 %multiply_bitcast_fusion.1 = f32[3072,512]{0,1:T(8,128)} fusion(f32[3072,512]{1,0:T(8,128)S(1)} %fusion.10, f32[3072,3072]{1,0:T(8,128)} %param.10, f32[3072]{0:T(1024)S(1)} %get-tuple-element.33), kind=kOutput, calls=%fused_computation.37 | convolution fusion | flops 28992602112 | bytes 50343936 | tf_op jit(solution)/shard_map/dot_general | solution.py:41
  222.4 0.0 reduce-scatter.7.cloned.1.call-start
  222.5 0.1 collective-permute-start.3
  222.5 35.5 %collective-permute-done.3 = f32[768,512]{1,0:T(8,128)S(1)} collective-permute-done((f32[768,512]{1,0:T(8,128)S(1)}, f32[768,512]{1,0:T(8,128)S(1)}, u32[]{:S(2)}, u32[]{:S(2)}) %collective-permute-start.3) | collective-permute-done | bytes 1572896 | tf_op jit(solution)/shard_map/ppermute | solution.py:35
  258.1 34.6 %collective-permute-done.4 = f32[768,512]{1,0:T(8,128)S(1)} collective-permute-done((f32[768,512]{1,0:T(8,128)S(1)}, f32[768,512]{1,0:T(8,128)S(1)}, u32[]{:S(2)}, u32[]{:S(2)}) %collective-permute-start.4) | collective-permute-done | bytes 1572896 | tf_op jit(solution)/shard_map/ppermute | solution.py:35
  292.7 1.1 copy-done.4
  293.8 32.7 %collective-permute-done.5 = f32[768,512]{1,0:T(8,128)} collective-permute-done((f32[768,512]{1,0:T(8,128)S(1)}, f32[768,512]{1,0:T(8,128)}, u32[]{:S(2)}, u32[]{:S(2)}) %collective-permute-start.5) | collective-permute-done | bytes 1572896 | tf_op jit(solution)/shard_map/ppermute | solution.py:35
  326.5 12.1 %fusion.3 = f32[3072,512]{1,0:T(8,128)S(1)} fusion(s32[]{:T(128)S(6)} %select_n.56, f32[768,512]{1,0:T(8,128)} %collective-permute-done.5, f32[768,512]{1,0:T(8,128)} %copy-done.4, f32[768,512]{1,0:T(8,128)S(1)} %collective-permute-done.3, f32[768,512]{1,0:T(8,128)S(1)} %get-tuple-element.38), kind=kLoop, calls=%fused_computation.21 | loop fusion | flops 11010048 | bytes 12582916 | tf_op jit(solution)/shard_map/jit(_roll_dynamic)/concatenate | solution.py:36
  338.6 2.6 copy-done.1
  341.3 66.3 %multiply_bitcast_fusion = f32[3072,512]{0,1:T(8,128)} fusion(f32[3072,512]{1,0:T(8,128)S(1)} %fusion.3, f32[3072,3072]{1,0:T(8,128)} %param.10, f32[3072]{0:T(1024)S(1)} %get-tuple-element.34), kind=kOutput, calls=%fused_computation.36 | convolution fusion | flops 28992602112 | bytes 50343936 | tf_op jit(solution)/shard_map/dot_general | solution.py:41
  407.6 0.0 all-gather.3.cloned.1.call-start
  407.7 3.8 fusion.20
  411.5 0.0 all-gather.5.cloned.1.call-start
  411.6 51.8 %reduce-scatter.7.cloned.1.call-done = f32[3072,128]{0,1:T(8,128)} async-done(((f32[3072,512]{0,1:T(8,128)}), f32[3072,128]{0,1:T(8,128)}) %reduce-scatter.7.cloned.1.call-update) | async-done | bytes 1572880 | tf_op jit(solution)/shard_map/reduce_scatter | solution.py:44
  463.4 3.4 fusion.21
  466.8 0.0 reduce-scatter.9.cloned.1.call-start
  466.9 44.4 %all-gather.3.cloned.1.call-done = f32[3072,512]{0,1:T(8,128)} async-done(((f32[3072,128]{0,1:T(8,128)}), f32[3072,512]{0,1:T(8,128)}) %all-gather.3.cloned.1.call-update) | async-done | bytes 6291472 | tf_op jit(solution)/shard_map/all_gather | solution.py:48
  511.4 14.7 %fusion.16 = f32[512,512]{1,0:T(8,128)} fusion(f32[3072,512]{0,1:T(8,128)} %all-gather.3.cloned.1.call-done, f32[3072,512]{1,0:T(8,128)} %copy-done, f32[]{:T(128)S(6)} %convert_element_type.11), kind=kOutput, calls=%fused_computation.34 | convolution fusion | flops 4833411072 | bytes 13631492 | tf_op jit(solution)/shard_map/dot_general | solution.py:50
  526.1 0.0 reduce-scatter.11.cloned.1.call-start
  526.1 33.6 %all-gather.5.cloned.1.call-done = f32[3072,512]{0,1:T(8,128)} async-done(((f32[3072,128]{0,1:T(8,128)}), f32[3072,512]{0,1:T(8,128)}) %all-gather.5.cloned.1.call-update) | async-done | bytes 6291472 | tf_op jit(solution)/shard_map/all_gather | solution.py:48
  559.8 14.6 %fusion.14 = f32[512,512]{1,0:T(8,128)} fusion(f32[3072,512]{0,1:T(8,128)} %all-gather.5.cloned.1.call-done, f32[3072,512]{1,0:T(8,128)} %copy-done.1, f32[]{:T(128)S(6)} %convert_element_type.11), kind=kOutput, calls=%fused_computation.32 | convolution fusion | flops 4833411072 | bytes 13631492 | tf_op jit(solution)/shard_map/dot_general | solution.py:50
  574.5 0.0 all-reduce.3.cloned.1.call-start
  574.5 12.6 %reduce-scatter.9.cloned.1.call-done = f32[512,128]{1,0:T(8,128)} async-done(((f32[512,512]{1,0:T(8,128)}), f32[512,128]{1,0:T(8,128)}) %reduce-scatter.9.cloned.1.call-update) | async-done | bytes 262160 | tf_op jit(solution)/shard_map/reduce_scatter | solution.py:58
  587.1 28.1 %reduce-scatter.11.cloned.1.call-done = f32[512,128]{1,0:T(8,128)} async-done(((f32[512,512]{1,0:T(8,128)}), f32[512,128]{1,0:T(8,128)}) %reduce-scatter.11.cloned.1.call-update) | async-done | bytes 262160 | tf_op jit(solution)/shard_map/reduce_scatter | solution.py:58
  615.2 2.1 pad_maximum_fusion
  617.3 2.4 copy.13
  619.6 36.4 %all-reduce.3.cloned.1.call-done = (f32[1,512,128]{2,1,0:T(8,128)}, f32[1,512,128]{2,1,0:T(8,128)}) async-done(((f32[1,512,128]{2,1,0:T(8,128)}, f32[1,512,128]{2,1,0:T(8,128)}), (f32[1,512,128]{2,1,0:T(8,128)}, f32[1,512,128]{2,1,0:T(8,128)})) %all-reduce.3.cloned.1.call-update) | async-done | bytes 524304 | tf_op jit(solution)/shard_map/psum | solution.py:58
  656.1 2.0 maximum_subtract_fusion
  (26 shorter events, 0.2 us)
Async XLA Ops:
  7.2 400.5 %reduce-scatter.5.cloned.1.call-start = ((), (), s32[]{:S(2)}) async-start(), calls=%async_computation.4 | async-start | bytes 7864320 | tf_op jit(solution)/shard_map/reduce_scatter | solution.py:44
  10.6 81.8 %copy-start.6 = (s32[2,128]{1,0:T(2,128)S(1)}, s32[2,128]{1,0:T(2,128)}, u32[]{:S(2)}) copy-start(s32[2,128]{1,0:T(2,128)} %param.13) | copy-start | bytes 3076
  10.6 82.0 %copy-start.5 = (s32[3072]{0:T(1024)S(1)}, s32[3072]{0:T(1024)}, u32[]{:S(2)}) copy-start(s32[3072]{0:T(1024)} %constant.233) | copy-start | bytes 36868
  13.1 1.2 copy-start.2
  14.3 39.4 %collective-permute-start = (f32[768,512]{1,0:T(8,128)S(1)}, f32[768,512]{1,0:T(8,128)S(1)}, u32[]{:S(2)}, u32[]{:S(2)}) collective-permute-start(f32[768,512]{1,0:T(8,128)S(1)} %get-tuple-element.37), channel_id=1, source_target_pairs={{0,4},{4,8},{8,12},{12,0},{1,5},{5,9},{9,13},{13,1},{2,6},{6,10},{... | collective-permute-start | bytes 4718600 | tf_op jit(solution)/shard_map/ppermute | solution.py:35
  53.7 1.1 copy-start.3
  54.9 37.5 %collective-permute-start.1 = (f32[768,512]{1,0:T(8,128)S(1)}, f32[768,512]{1,0:T(8,128)}, u32[]{:S(2)}, u32[]{:S(2)}) collective-permute-start(f32[768,512]{1,0:T(8,128)S(1)} %collective-permute-done), channel_id=1, source_target_pairs={{0,4},{4,8},{8,12},{12,0},{1,5},{5,9},{9,13},{13,1},{2,6},{6,10},{... | collective-permute-start | bytes 4718600 | tf_op jit(solution)/shard_map/ppermute | solution.py:35
  92.3 36.8 %collective-permute-start.2 = (f32[768,512]{1,0:T(8,128)}, f32[768,512]{1,0:T(8,128)}, u32[]{:S(2)}, u32[]{:S(2)}) collective-permute-start(f32[768,512]{1,0:T(8,128)} %collective-permute-done.1), channel_id=1, source_target_pairs={{0,4},{4,8},{8,12},{12,0},{1,5},{5,9},{9,13},{13,1},{2,6},{6,10},{... | collective-permute-start | bytes 4718600 | tf_op jit(solution)/shard_map/ppermute | solution.py:35
  139.6 2.6 copy-start
  222.4 241.0 %reduce-scatter.7.cloned.1.call-start = ((), (), s32[]{:S(2)}) async-start(), calls=%async_computation.5 | async-start | bytes 7864320 | tf_op jit(solution)/shard_map/reduce_scatter | solution.py:44
  222.5 35.6 %collective-permute-start.3 = (f32[768,512]{1,0:T(8,128)S(1)}, f32[768,512]{1,0:T(8,128)S(1)}, u32[]{:S(2)}, u32[]{:S(2)}) collective-permute-start(f32[768,512]{1,0:T(8,128)S(1)} %get-tuple-element.38), channel_id=1, source_target_pairs={{0,4},{4,8},{8,12},{12,0},{1,5},{5,9},{9,13},{13,1},{2,6},{6,10},{... | collective-permute-start | bytes 4718600 | tf_op jit(solution)/shard_map/ppermute | solution.py:35
  258.1 34.6 %collective-permute-start.4 = (f32[768,512]{1,0:T(8,128)S(1)}, f32[768,512]{1,0:T(8,128)S(1)}, u32[]{:S(2)}, u32[]{:S(2)}) collective-permute-start(f32[768,512]{1,0:T(8,128)S(1)} %collective-permute-done.3), channel_id=1, source_target_pairs={{0,4},{4,8},{8,12},{12,0},{1,5},{5,9},{9,13},{13,1},{2,6},{6,10},{... | collective-permute-start | bytes 4718600 | tf_op jit(solution)/shard_map/ppermute | solution.py:35
  292.7 1.1 copy-start.4
  292.7 33.8 %collective-permute-start.5 = (f32[768,512]{1,0:T(8,128)S(1)}, f32[768,512]{1,0:T(8,128)}, u32[]{:S(2)}, u32[]{:S(2)}) collective-permute-start(f32[768,512]{1,0:T(8,128)S(1)} %collective-permute-done.4), channel_id=1, source_target_pairs={{0,4},{4,8},{8,12},{12,0},{1,5},{5,9},{9,13},{13,1},{2,6},{6,10},{... | collective-permute-start | bytes 4718600 | tf_op jit(solution)/shard_map/ppermute | solution.py:35
  338.6 2.6 copy-start.1
  407.6 103.7 %all-gather.3.cloned.1.call-start = ((), (), s32[]{:S(2)}) async-start(), calls=%async_computation.6 | async-start | bytes 7864320 | tf_op jit(solution)/shard_map/all_gather | solution.py:48
  411.5 148.3 %all-gather.5.cloned.1.call-start = ((), (), s32[]{:S(2)}) async-start(), calls=%async_computation.8 | async-start | bytes 7864320 | tf_op jit(solution)/shard_map/all_gather | solution.py:48
  466.8 120.3 %reduce-scatter.9.cloned.1.call-start = ((), (), s32[]{:S(2)}) async-start(), calls=%async_computation.7 | async-start | bytes 1310720 | tf_op jit(solution)/shard_map/reduce_scatter | solution.py:58
  526.1 89.1 %reduce-scatter.11.cloned.1.call-start = ((), (), s32[]{:S(2)}) async-start(), calls=%async_computation.9 | async-start | bytes 1310720 | tf_op jit(solution)/shard_map/reduce_scatter | solution.py:58
  574.5 81.6 %all-reduce.3.cloned.1.call-start = ((), (), s32[]{:S(2)}) async-start(), calls=%async_computation.10 | async-start | bytes 1048576 | tf_op jit(solution)/shard_map/psum | solution.py:58
Sparse Core Ops, SparseCore 0:
  222.5 56.0 reduce-scatter.4
  407.8 55.5 reduce-scatter.6
  465.0 46.3 all-gather.2
  513.4 46.3 all-gather.4
  562.1 24.9 reduce-scatter.8
  590.2 24.8 reduce-scatter.10
  617.6 38.4 all-reduce.2
